TPU v7x, 32 devices: a whole 2x2x4 slice. The times are simulated.
32 devices in a mesh: grp: 2 (over y), epoch: 4 (over z), tile: 2 (over x), sub: 2 (over core).
Axes of the slice: x: 2, y: 2, z: 4, core: 2. Of those that a mesh axis runs over, the one named last changes fastest.
Arguments:
- epoch_images: float32 [32, 512, 512], P(('grp', 'epoch'), ('tile', 'sub')), parts along dimension 0, may hold values from -8 to 8
- psf_bank: float32 [16, 16, 16], replicated, may hold values from 0.05 to 1
- psf_index: int32 [32], P(('grp', 'epoch')), parts along dimension 0, may hold values from 0 to 15
- flux_scale: float32 [32], P(('grp', 'epoch')), parts along dimension 0, may hold values from 0.3 to 3
- noise_level: float32 [32], P(('grp', 'epoch')), parts along dimension 0, may hold values from 0.5 to 2
- src_row: int32 [8192], P('grp'), parts along dimension 0, may hold values from 0 to 511
- src_col: int32 [8192], P('grp'), parts along dimension 0, may hold values from 0 to 511
Outputs:
- difference: float32 [32, 512, 512], P(('grp', 'epoch'), ('tile', 'sub')), parts along dimension 0
- fluxes: float32 [32, 4096], P(('grp', 'epoch'), ('tile', 'sub')), parts along dimension 0
There are 2 independent parts, one for each index of `grp`. A program takes and returns all parts, laid end to end along the dimension named above; an argument that names none is the same for every part. Nothing has to cross between parts.
All inputs are finite; a program needn't handle non-finite values.
Results may differ from a plain program's by a relative error of at most 0.0003.
Values sent between devices are 32-bit elements; how exact they have to be, the bound alone decides.
A program may use at most 128 MiB of HBM per device.

v0:
```python
import functools
import math

import jax
import jax.numpy as jnp
import numpy as np
from jax import lax
from jax.experimental import pallas as pl
from jax.experimental.pallas import tpu as pltpu
from jax.sharding import PartitionSpec as P

reg_floor = 0.01
MESH = pl.DeviceIdType.MESH
pad_rows = 8


def halves(table):
    table = jnp.asarray(table, jnp.float32)
    high = table.astype(jnp.bfloat16)
    return high, (table - high.astype(jnp.float32)).astype(jnp.bfloat16)


def trig(first, second, length):
    angle = (np.outer(first, second) % length) * (2.0 * math.pi / length)
    return np.cos(angle), np.sin(angle)


def numpy_halves(table):
    table = np.asarray(table, np.float32)
    high = table.astype(jnp.bfloat16)
    return high, (table - high.astype(np.float32)).astype(jnp.bfloat16)


def make_tables(side, slabs, stamp):
    block = side // (2 * slabs)
    whole = np.arange(side)
    rows = []
    stamp_cols = []
    offsets = np.arange(stamp) - stamp // 2
    for slab in range(slabs):
        freq = slab * block + np.arange(block)
        cosine, sine = trig(freq, whole, side)
        sine = -sine
        if slab == 0:
            sine[0] = np.where(whole % 2 == 0, 1.0, -1.0)
        rows += [cosine, sine]
        cosine, sine = trig(freq, offsets, side)
        extra_re = np.zeros((pad_rows, stamp))
        extra_im = np.zeros((pad_rows, stamp))
        if slab == 0:
            nyq_cos, nyq_sin = trig(np.array([side // 2]), offsets, side)
            extra_re[0] = nyq_cos[0]
            extra_im[0] = -nyq_sin[0]
        stamp_cols.append(np.concatenate([cosine, extra_re, -sine, extra_im]))
    row_hi, row_lo = numpy_halves(np.concatenate(rows))
    cosine, sine = trig(whole, whole, side)
    col_hi, col_lo = numpy_halves(np.concatenate([cosine, sine], axis=1))
    cosine, sine = trig(offsets, whole, side)
    hi, lo = numpy_halves(np.concatenate([cosine, sine], axis=1))
    stamp_rows = np.concatenate([hi, hi, lo])
    return row_hi, row_lo, col_hi, col_lo, np.stack(stamp_cols).astype(np.float32), stamp_rows


def split(value):
    high = value.astype(jnp.bfloat16)
    return high, (value - high.astype(jnp.float32)).astype(jnp.bfloat16)


def mul(left, right, contract=((1,), (0,))):
    return lax.dot_general(left, right, (contract, ((), ())), preferred_element_type=jnp.float32)


def kernel(
    slabs, subs, groups, img, bank, index, flux, noise, srow, scol,
    row_hi, row_lo, col_hi, col_lo, stamp_cols, stamp_rows,
    diff_out, flux_out,
    fwd_send, fwd_recv, bwd_send, bwd_recv, spec, filt_hi, filt_lo, psf, inv_sq, weight_own, weight_recv,
    quot, part, part_recv, block, full, pick_row, pick_tab, fl_send, fl_recv,
    s_fs, s_fr, s_bs, s_br, s_ws, s_wr, s_rs, s_rr, s_as, s_ar, s_xs, s_xr,
):
    f32 = jnp.float32
    epochs, slab_rows, side = img.shape
    stamps = bank.shape[0]
    half = side // (2 * slabs)
    ext = half + pad_rows
    width = side // groups
    per_dest = fl_send.shape[2]
    chunk = min(512, per_dest)
    chunks = per_dest // chunk
    tile = lax.axis_index("tile")
    sub = lax.axis_index("sub")
    me = tile * subs + sub
    zed = lax.axis_index("epoch")

    def slab_peer(step):
        other = lax.rem(me + step, slabs)
        return other, {"tile": other // subs, "sub": lax.rem(other, subs)}

    def zed_peer(step):
        other = lax.rem(zed + step, groups)
        return other, {"epoch": other}

    slab_order = sorted(range(1, slabs), key=lambda step: step % subs == 0, reverse=True)
    slab_order = [s for s in slab_order]

    barrier = pltpu.get_barrier_semaphore()
    for step in range(1, slabs):
        pl.semaphore_signal(barrier, inc=1, device_id=slab_peer(step)[1], device_id_type=MESH)
    for step in range(1, groups):
        pl.semaphore_signal(barrier, inc=1, device_id=zed_peer(step)[1], device_id_type=MESH)

    for e in range(epochs):
        hi, lo = split(img[e])
        nt = ((1,), (1,))
        fwd = mul(row_hi[...], hi, nt) + mul(row_hi[...], lo, nt) + mul(row_lo[...], hi, nt)
        fwd_send[e] = fwd.reshape(slabs, 2 * half, slab_rows)
        if e == 0:
            pl.semaphore_wait(barrier, slabs - 1 + groups - 1)
        for step in slab_order:
            other, where = slab_peer(step)
            pltpu.make_async_remote_copy(
                src_ref=fwd_send.at[e, other], dst_ref=fwd_recv.at[e, me],
                send_sem=s_fs.at[step, e], recv_sem=s_fr.at[step, e],
                device_id=where, device_id_type=MESH,
            ).start()
        fwd_recv[e, me] = fwd_send[e, me]

    lane = lax.broadcasted_iota(jnp.int32, (8, 128), 1)
    wsum = jnp.zeros((8, 128), f32)
    for e in range(epochs):
        ratio = jnp.full((8, 128), flux[e], f32) / jnp.full((8, 128), noise[e], f32)
        wsum = wsum + jnp.where(lane == index[e], ratio * ratio, 0.0)
    weight_own[...] = wsum
    for step in range(1, groups):
        _, where = zed_peer(step)
        pltpu.make_async_remote_copy(
            src_ref=weight_own, dst_ref=weight_recv.at[step],
            send_sem=s_ws.at[step], recv_sem=s_wr.at[step], device_id=where, device_id_type=MESH,
        ).start()

    cols = stamp_cols[me]
    group_lane = lax.broadcasted_iota(jnp.int32, (2 * ext, 3 * bank.shape[1]), 1)
    middle = (group_lane >= bank.shape[1]) & (group_lane < 2 * bank.shape[1])

    def stamp_body(k, carry):
        stamp = bank[k]
        total = jnp.sum(jnp.sum(stamp, axis=1, keepdims=True), axis=0, keepdims=True)
        stamp = stamp / total
        square = jnp.sum(jnp.sum(stamp * stamp, axis=1, keepdims=True), axis=0, keepdims=True)
        inv_sq[k] = jnp.broadcast_to(1.0 / square, (8, 128))
        wide = jnp.concatenate([stamp, stamp, stamp], axis=0)
        part_spec = lax.dot_general(
            cols, wide, (((1,), (1,)), ((), ())), precision=lax.Precision.HIGHEST, preferred_element_type=f32
        )
        high = part_spec.astype(jnp.bfloat16).astype(f32)
        left = jnp.where(middle, part_spec - high, high).astype(jnp.bfloat16)
        both = mul(left, stamp_rows[...])
        psf[k, 0] = both[:ext, :side] + both[ext:, side:]
        psf[k, 1] = both[ext:, :side] - both[:ext, side:]
        return carry

    lax.fori_loop(0, stamps, stamp_body, 0)

    for step in range(1, groups):
        _, where = zed_peer(step)
        pltpu.make_async_remote_copy(
            src_ref=weight_own, dst_ref=weight_recv.at[step],
            send_sem=s_ws.at[step], recv_sem=s_wr.at[step], device_id=where, device_id_type=MESH,
        ).wait()
        wsum = wsum + weight_recv[step]
    total_q = jnp.full((ext, side), reg_floor, f32)
    for k in range(stamps):
        re = psf[k, 0]
        im = psf[k, 1]
        total_q = total_q + wsum[0:1, k : k + 1] * (re * re + im * im)
    quot[0] = total_q
    quot[1] = jnp.sqrt(total_q)

    mine = pl.ds(pl.multiple_of(me * 2 * half, 2 * half), 2 * half)
    pixel = lax.broadcasted_iota(jnp.int32, (side, chunk), 0)

    def pick_body(c, carry):
        at = pl.ds(pl.multiple_of(c * chunk, chunk), chunk)
        pick_row[c] = jnp.where(pixel == srow[:, at], 1.0, 0.0).astype(jnp.bfloat16)
        hot = jnp.where(pixel == scol[:, at], 1.0, 0.0).astype(jnp.bfloat16)
        pick_tab[c] = mul(row_hi[mine, :], hot) + mul(row_lo[mine, :], hot)
        return carry

    lax.fori_loop(0, chunks * slabs, pick_body, 0)

    first = (lax.broadcasted_iota(jnp.int32, (half, side), 0) == 0) & (me == 0)
    first_ext = (lax.broadcasted_iota(jnp.int32, (pad_rows, side), 0) == 0) & (me == 0)
    zero_pad = jnp.zeros((pad_rows, side), f32)
    num_re = jnp.zeros((ext, side), f32)
    num_im = jnp.zeros((ext, side), f32)
    for e in range(epochs):
        for step in slab_order:
            other, where = slab_peer(step)
            pltpu.make_async_remote_copy(
                src_ref=fwd_send.at[e, other], dst_ref=fwd_recv.at[e, me],
                send_sem=s_fs.at[step, e], recv_sem=s_fr.at[step, e],
                device_id=where, device_id_type=MESH,
            ).wait()
        if slab_rows % 128 == 0:
            pieces = [(0, side, jnp.concatenate([fwd_recv[e, s] for s in range(slabs)], axis=1))]
        else:
            pieces = [(s * slab_rows, slab_rows, fwd_recv[e, s]) for s in range(slabs)]
        both = None
        for start, size, value in pieces:
            hi, lo = split(value)
            high_tab = col_hi[start : start + size, :]
            term = mul(hi, high_tab) + mul(lo, high_tab) + mul(hi, col_lo[start : start + size, :])
            both = term if both is None else both + term
        a_re, b_re = both[:half, :side], both[:half, side:]
        a_im, b_im = both[half:, :side], both[half:, side:]
        img_re = jnp.concatenate(
            [a_re + jnp.where(first, 0.0, b_im), jnp.where(first_ext, a_im[:pad_rows], zero_pad)], axis=0
        )
        img_im = jnp.concatenate(
            [jnp.where(first, 0.0, a_im) - b_re, jnp.where(first_ext, -b_im[:pad_rows], zero_pad)], axis=0
        )
        spec[e, 0] = img_re
        spec[e, 1] = img_im
        psf_re = psf[index[e], 0]
        psf_im = psf[index[e], 1]
        sig = jnp.full((1, side), noise[e], f32)
        weight = jnp.full((1, side), flux[e], f32) / (sig * sig)
        num_re = num_re + weight * (psf_re * img_re + psf_im * img_im)
        num_im = num_im + weight * (psf_re * img_im - psf_im * img_re)

    for g in range(groups):
        part[g, 0] = num_re[:, g * width : (g + 1) * width]
        part[g, 1] = num_im[:, g * width : (g + 1) * width]
    for step in range(1, groups):
        other, where = zed_peer(step)
        pltpu.make_async_remote_copy(
            src_ref=part.at[other], dst_ref=part_recv.at[step],
            send_sem=s_rs.at[step], recv_sem=s_rr.at[step], device_id=where, device_id_type=MESH,
        ).start()
    total = part[zed]
    for step in range(1, groups):
        other, where = zed_peer(step)
        pltpu.make_async_remote_copy(
            src_ref=part.at[other], dst_ref=part_recv.at[step],
            send_sem=s_rs.at[step], recv_sem=s_rr.at[step], device_id=where, device_id_type=MESH,
        ).wait()
        total = total + part_recv[step]
    block[...] = total
    for step in range(1, groups):
        other, where = zed_peer(step)
        pltpu.make_async_remote_copy(
            src_ref=block, dst_ref=full.at[zed],
            send_sem=s_as.at[step], recv_sem=s_ar.at[step], device_id=where, device_id_type=MESH,
        ).start()
    full[zed] = total
    for step in range(1, groups):
        other, where = zed_peer(step)
        pltpu.make_async_remote_copy(
            src_ref=block, dst_ref=full.at[zed],
            send_sem=s_as.at[step], recv_sem=s_ar.at[step], device_id=where, device_id_type=MESH,
        ).wait()
    root_q = quot[1]
    inv_root = 1.0 / root_q
    templ_re = jnp.concatenate([full[g, 0] for g in range(groups)], axis=1) * inv_root
    templ_im = jnp.concatenate([full[g, 1] for g in range(groups)], axis=1) * inv_root

    line = lax.broadcasted_iota(jnp.int32, (ext, side), 0)
    single = ((line == 0) & (me == 0)) | (line >= half)
    norm = jnp.where(single, 1.0 / (side * side), 2.0 / (side * side))

    def back(value_re, value_im):
        hi, lo = split(jnp.concatenate([value_re, value_im], axis=0))
        both = mul(hi, col_hi[...]) + mul(lo, col_hi[...]) + mul(hi, col_lo[...])
        g_re = both[:ext, :side] - both[ext:, side:]
        g_im = both[ext:, :side] + both[:ext, side:]
        nyq = g_re[half:, :]
        head = jnp.where(first_ext, nyq, g_im[:pad_rows])
        return jnp.concatenate([g_re[:half], head, g_im[pad_rows:half]], axis=0)

    for e in range(epochs):
        psf_re = psf[index[e], 0]
        psf_im = psf[index[e], 1]
        img_re = spec[e, 0]
        img_im = spec[e, 1]
        sig = jnp.full((1, side), noise[e], f32)
        scale = jnp.full((1, side), flux[e], f32)
        power = psf_re * psf_re + psf_im * psf_im
        inv = norm / jnp.sqrt(sig * sig * quot[0] + scale * scale * power + reg_floor)
        d_re = (root_q * img_re - scale * (psf_re * templ_re - psf_im * templ_im)) * inv
        d_im = (root_q * img_im - scale * (psf_re * templ_im + psf_im * templ_re)) * inv
        spec[e, 0] = d_re
        spec[e, 1] = d_im
        planes = back(d_re, d_im)
        for s in range(slabs):
            bwd_send[e, s] = planes[:, s * slab_rows : (s + 1) * slab_rows]
        for step in slab_order:
            other, where = slab_peer(step)
            pltpu.make_async_remote_copy(
                src_ref=bwd_send.at[e, other], dst_ref=bwd_recv.at[e, me],
                send_sem=s_bs.at[step, e], recv_sem=s_br.at[step, e],
                device_id=where, device_id_type=MESH,
            ).start()
        bwd_recv[e, me] = bwd_send[e, me]

    for e in range(epochs):
        psf_re = psf[index[e], 0]
        psf_im = psf[index[e], 1]
        d_re = spec[e, 0]
        d_im = spec[e, 1]
        inv = inv_sq[index[e]][0:1, 0:1]
        hi, lo = split(back((d_re * psf_re + d_im * psf_im) * inv, (d_im * psf_re - d_re * psf_im) * inv))
        filt_hi[e * 2 * half : (e + 1) * 2 * half, :] = hi
        filt_lo[e * 2 * half : (e + 1) * 2 * half, :] = lo

    def flux_body(c, carry):
        got = mul(filt_hi[...], pick_row[c]) + mul(filt_lo[...], pick_row[c])
        got = got.reshape(epochs, 2 * half, chunk) * pick_tab[c][None]
        fl_send[c // chunks, :, pl.ds(pl.multiple_of(lax.rem(c, chunks) * chunk, chunk), chunk)] = jnp.sum(got, axis=1)
        return carry

    lax.fori_loop(0, chunks * slabs, flux_body, 0)
    for step in slab_order:
        other, where = slab_peer(step)
        pltpu.make_async_remote_copy(
            src_ref=fl_send.at[other], dst_ref=fl_recv.at[step],
            send_sem=s_xs.at[step], recv_sem=s_xr.at[step], device_id=where, device_id_type=MESH,
        ).start()

    for e in range(epochs):
        for step in slab_order:
            other, where = slab_peer(step)
            pltpu.make_async_remote_copy(
                src_ref=bwd_send.at[e, other], dst_ref=bwd_recv.at[e, me],
                send_sem=s_bs.at[step, e], recv_sem=s_br.at[step, e],
                device_id=where, device_id_type=MESH,
            ).wait()
        hi, lo = split(bwd_recv[e].reshape(side, slab_rows))
        tn = ((0,), (0,))
        diff_out[e] = mul(hi, row_hi[...], tn) + mul(lo, row_hi[...], tn) + mul(hi, row_lo[...], tn)

    total = fl_send[me]
    for step in slab_order:
        other, where = slab_peer(step)
        pltpu.make_async_remote_copy(
            src_ref=fl_send.at[other], dst_ref=fl_recv.at[step],
            send_sem=s_xs.at[step], recv_sem=s_xr.at[step], device_id=where, device_id_type=MESH,
        ).wait()
        total = total + fl_recv[step]
    flux_out[...] = total


def shards(slabs, subs, groups, tables, images, bank, index, flux, noise, src_row, src_col):
    epochs, slab_rows, side = images.shape
    stamps, stamp, _ = bank.shape
    sources = src_row.shape[0]
    half = side // (2 * slabs)
    ext = half + pad_rows
    width = side // groups
    per_dest = sources // slabs
    chunk = min(512, per_dest)
    f32 = jnp.float32
    vmem = pl.BlockSpec(memory_space=pltpu.VMEM)
    smem = pl.BlockSpec(memory_space=pltpu.SMEM)
    dma = pltpu.SemaphoreType.DMA
    plane = pltpu.VMEM((epochs, slabs, 2 * half, slab_rows), f32)
    return pl.pallas_call(
        functools.partial(kernel, slabs, subs, groups),
        out_shape=(
            jax.ShapeDtypeStruct((epochs, slab_rows, side), f32),
            jax.ShapeDtypeStruct((epochs, per_dest), f32),
        ),
        in_specs=[vmem, vmem, smem, smem, smem] + [vmem] * 8,
        out_specs=(vmem, vmem),
        scratch_shapes=[
            plane, plane, plane, plane,
            pltpu.VMEM((epochs, 2, ext, side), f32),
            pltpu.VMEM((epochs * 2 * half, side), jnp.bfloat16),
            pltpu.VMEM((epochs * 2 * half, side), jnp.bfloat16),
            pltpu.VMEM((stamps, 2, ext, side), f32),
            pltpu.VMEM((stamps, 8, 128), f32),
            pltpu.VMEM((8, 128), f32),
            pltpu.VMEM((groups, 8, 128), f32),
            pltpu.VMEM((2, ext, side), f32),
            pltpu.VMEM((groups, 2, ext, width), f32),
            pltpu.VMEM((groups, 2, ext, width), f32),
            pltpu.VMEM((2, ext, width), f32),
            pltpu.VMEM((groups, 2, ext, width), f32),
            pltpu.VMEM((sources // chunk, side, chunk), jnp.bfloat16),
            pltpu.VMEM((sources // chunk, 2 * half, chunk), f32),
            pltpu.VMEM((slabs, epochs, per_dest), f32),
            pltpu.VMEM((slabs, epochs, per_dest), f32),
            dma((slabs, epochs)), dma((slabs, epochs)), dma((slabs, epochs)), dma((slabs, epochs)),
            dma((groups,)), dma((groups,)), dma((groups,)), dma((groups,)), dma((groups,)), dma((groups,)),
            dma((slabs,)), dma((slabs,)),
        ],
        compiler_params=pltpu.CompilerParams(
            collective_id=0, has_side_effects=True, vmem_limit_bytes=60 * 1024 * 1024
        ),
        name="zogy",
    )(images, bank, index, flux, noise, src_row.reshape(1, sources), src_col.reshape(1, sources), *tables)


def solution(mesh):
    subs = mesh.shape["sub"]
    slabs = mesh.shape["tile"] * subs
    groups = mesh.shape["epoch"]
    in_specs = (
        P(("grp", "epoch"), ("tile", "sub"), None),
        P(),
        P(("grp", "epoch")),
        P(("grp", "epoch")),
        P(("grp", "epoch")),
        P("grp"),
        P("grp"),
    )
    out_specs = (P(("grp", "epoch"), ("tile", "sub"), None), P(("grp", "epoch"), ("tile", "sub")))

    def run(images, bank, index, flux, noise, src_row, src_col):
        tables = make_tables(images.shape[2], slabs, bank.shape[1])
        body = functools.partial(shards, slabs, subs, groups, tables)
        return jax.shard_map(body, mesh=mesh, in_specs=in_specs, out_specs=out_specs, check_vma=False)(
            images, bank, index, flux, noise, src_row, src_col
        )

    return run
```

profile of v0, /device:TPU:0, one launch (start us, length us, event | category | flops | bytes accessed | tf_op | source)
XLA Modules:
  0.0 59.5 jit_solution(6521629833691272274)
XLA Ops:
  0.6 56.0 %zogy.1 = (f32[4,128,512]{2,1,0:T(8,128)}, f32[4,1024]{1,0:T(4,128)}) custom-call(f32[4,128,512]{2,1,0:T(8,128)} %img.1, f32[16,16,16]{2,1,0:T(8,128)} %bank.1, s32[4]{0:T(128)} %index.1, f32[4]{0:T(128)} %flux.1, f32[4]{0:T(128)} %noise.1, s32[1,4096]{1,0:T(1,128)} %bitcast.2, s32[1,4096]{1,0:T(1,128)} %bitcast.3, bf16[512,512]{1,0:T(8,128)(2,1)} %constant.12.clone.row_hi, ...), custom_call_target="tpu_custom_call" | custom-call | tf_op jit(solution)/shard_map/zogy/pallas_call | solution.py:366
  56.6 0.0 copy-start
  56.7 2.3 %copy.17 = f32[4,128,512]{2,1,0:T(8,128)} copy(f32[4,128,512]{2,1,0:T(8,128)} %get-tuple-element.4) | data formatting | bytes 2097152
  58.9 0.0 copy-done
  58.9 0.6 %copy.18 = f32[4,1024]{1,0:T(4,128)} copy(f32[4,1024]{1,0:T(4,128)S(1)} %copy-done) | data formatting | bytes 32768
Async XLA Ops:
  56.6 2.3 %copy-start = (f32[4,1024]{1,0:T(4,128)S(1)}, f32[4,1024]{1,0:T(4,128)}, u32[]{:S(2)}) copy-start(f32[4,1024]{1,0:T(4,128)} %get-tuple-element.5) | copy-start | bytes 49156
where the time goes:
time: 59.7 us; the launch traced here: 59.5 us
  Pallas kernels  56 us (94%)
  local copies, waits for them, and re-layouts  2.88 us (5%)
  between operations  0.65 us (1%)
    pallas_call x1, Pallas kernels, shards(): pl.pallas_call(functools.partial(kernel, slabs, subs, groups), out_shape=...  56 us
    unnamed x4, local copies, waits for them, and re-layouts  2.88 us

commit v1 on v0

--- a/solution.py
+++ b/solution.py
@@ -139,27 +139,37 @@
         ).start()
 
     cols = stamp_cols[me]
-    group_lane = lax.broadcasted_iota(jnp.int32, (2 * ext, 3 * bank.shape[1]), 1)
+    batch = 4 if stamps % 4 == 0 else 1
+    group_lane = lax.broadcasted_iota(jnp.int32, (batch * 2 * ext, 3 * bank.shape[1]), 1)
     middle = (group_lane >= bank.shape[1]) & (group_lane < 2 * bank.shape[1])
 
-    def stamp_body(k, carry):
-        stamp = bank[k]
-        total = jnp.sum(jnp.sum(stamp, axis=1, keepdims=True), axis=0, keepdims=True)
-        stamp = stamp / total
-        square = jnp.sum(jnp.sum(stamp * stamp, axis=1, keepdims=True), axis=0, keepdims=True)
-        inv_sq[k] = jnp.broadcast_to(1.0 / square, (8, 128))
-        wide = jnp.concatenate([stamp, stamp, stamp], axis=0)
-        part_spec = lax.dot_general(
-            cols, wide, (((1,), (1,)), ((), ())), precision=lax.Precision.HIGHEST, preferred_element_type=f32
-        )
+    def stamp_body(group, carry):
+        parts = []
+        for i in range(batch):
+            k = group * batch + i
+            stamp = bank[k]
+            total = jnp.sum(jnp.sum(stamp, axis=1, keepdims=True), axis=0, keepdims=True)
+            stamp = stamp / total
+            square = jnp.sum(jnp.sum(stamp * stamp, axis=1, keepdims=True), axis=0, keepdims=True)
+            inv_sq[k] = jnp.broadcast_to(1.0 / square, (8, 128))
+            wide = jnp.concatenate([stamp, stamp, stamp], axis=0)
+            parts.append(
+                lax.dot_general(
+                    cols, wide, (((1,), (1,)), ((), ())),
+                    precision=lax.Precision.HIGHEST, preferred_element_type=f32,
+                )
+            )
+        part_spec = jnp.concatenate(parts, axis=0)
         high = part_spec.astype(jnp.bfloat16).astype(f32)
         left = jnp.where(middle, part_spec - high, high).astype(jnp.bfloat16)
-        both = mul(left, stamp_rows[...])
-        psf[k, 0] = both[:ext, :side] + both[ext:, side:]
-        psf[k, 1] = both[ext:, :side] - both[:ext, side:]
+        every = mul(left, stamp_rows[...])
+        for i in range(batch):
+            both = every[i * 2 * ext : (i + 1) * 2 * ext]
+            psf[group * batch + i, 0] = both[:ext, :side] + both[ext:, side:]
+            psf[group * batch + i, 1] = both[ext:, :side] - both[:ext, side:]
         return carry
 
-    lax.fori_loop(0, stamps, stamp_body, 0)
+    lax.fori_loop(0, stamps // batch, stamp_body, 0)
 
     for step in range(1, groups):
         _, where = zed_peer(step)
@@ -186,7 +196,7 @@
         pick_tab[c] = mul(row_hi[mine, :], hot) + mul(row_lo[mine, :], hot)
         return carry
 
-    lax.fori_loop(0, chunks * slabs, pick_body, 0)
+    picks = chunks * slabs
 
     first = (lax.broadcasted_iota(jnp.int32, (half, side), 0) == 0) & (me == 0)
     first_ext = (lax.broadcasted_iota(jnp.int32, (pad_rows, side), 0) == 0) & (me == 0)
@@ -237,6 +247,7 @@
             src_ref=part.at[other], dst_ref=part_recv.at[step],
             send_sem=s_rs.at[step], recv_sem=s_rr.at[step], device_id=where, device_id_type=MESH,
         ).start()
+    lax.fori_loop(0, picks // 2, pick_body, 0)
     total = part[zed]
     for step in range(1, groups):
         other, where = zed_peer(step)
@@ -253,6 +264,7 @@
             send_sem=s_as.at[step], recv_sem=s_ar.at[step], device_id=where, device_id_type=MESH,
         ).start()
     full[zed] = total
+    lax.fori_loop(picks // 2, picks, pick_body, 0)
     for step in range(1, groups):
         other, where = zed_peer(step)
         pltpu.make_async_remote_copy(

time: 59.7 us -> 54 us (0.905)
  Pallas kernels: 56 us -> 50.3 us
    pallas_call x1, Pallas kernels: 56 us -> 50.3 us  [shards(): pl.pallas_call(functools.partial(kernel, slabs, subs, groups), out_shape=...]
where the time goes in v1:
time: 54 us; the launch traced here: 53.8 us
  Pallas kernels  50.3 us (93%)
  local copies, waits for them, and re-layouts  2.88 us (5%)
  between operations  0.65 us (1%)
    pallas_call x1, Pallas kernels, shards(): pl.pallas_call(functools.partial(kernel, slabs, subs, groups), out_shape=...  50.3 us
    unnamed x4, local copies, waits for them, and re-layouts  2.88 us

profile of v1, /device:TPU:0, one launch (start us, length us, event | category | flops | bytes accessed | tf_op | source)
XLA Modules:
  0.0 53.8 jit_solution(8163139637229229608)
XLA Ops:
  0.6 50.3 %zogy.1 = (f32[4,128,512]{2,1,0:T(8,128)}, f32[4,1024]{1,0:T(4,128)}) custom-call(f32[4,128,512]{2,1,0:T(8,128)} %img.1, f32[16,16,16]{2,1,0:T(8,128)} %bank.1, s32[4]{0:T(128)} %index.1, f32[4]{0:T(128)} %flux.1, f32[4]{0:T(128)} %noise.1, s32[1,4096]{1,0:T(1,128)} %bitcast.2, s32[1,4096]{1,0:T(1,128)} %bitcast.3, bf16[512,512]{1,0:T(8,128)(2,1)} %constant.12.clone.row_hi, ...), custom_call_target="tpu_custom_call" | custom-call | tf_op jit(solution)/shard_map/zogy/pallas_call | solution.py:378
  51.0 0.0 copy-start
  51.0 2.3 %copy.17 = f32[4,128,512]{2,1,0:T(8,128)} copy(f32[4,128,512]{2,1,0:T(8,128)} %get-tuple-element.4) | data formatting | bytes 2097152
  53.2 0.0 copy-done
  53.2 0.6 %copy.18 = f32[4,1024]{1,0:T(4,128)} copy(f32[4,1024]{1,0:T(4,128)S(1)} %copy-done) | data formatting | bytes 32768
Async XLA Ops:
  51.0 2.3 %copy-start = (f32[4,1024]{1,0:T(4,128)S(1)}, f32[4,1024]{1,0:T(4,128)}, u32[]{:S(2)}) copy-start(f32[4,1024]{1,0:T(4,128)} %get-tuple-element.5) | copy-start | bytes 49156

commit v2 on v1

v2 whole, which is shorter than its diff:
```python
import functools
import math

import jax
import jax.numpy as jnp
import numpy as np
from jax import lax
from jax.experimental import pallas as pl
from jax.experimental.pallas import tpu as pltpu
from jax.sharding import PartitionSpec as P

reg_floor = 0.01
MESH = pl.DeviceIdType.MESH
pad_rows = 8
strips = 2


def trig(first, second, length):
    angle = (np.outer(first, second) % length) * (2.0 * math.pi / length)
    return np.cos(angle), np.sin(angle)


def numpy_halves(table):
    table = np.asarray(table, np.float32)
    high = table.astype(jnp.bfloat16)
    return high, (table - high.astype(np.float32)).astype(jnp.bfloat16)


def make_tables(side, slabs, stamp):
    strip = side // (2 * slabs * strips)
    whole = np.arange(side)
    offsets = np.arange(stamp) - stamp // 2
    rows = [[] for _ in range(strips)]
    stamp_cols = []
    for slab in range(slabs):
        own = []
        for h in range(strips):
            freq = (slab * strips + h) * strip + np.arange(strip)
            cosine, sine = trig(freq, whole, side)
            sine = -sine
            if slab == 0 and h == 0:
                sine[0] = np.where(whole % 2 == 0, 1.0, -1.0)
            rows[h] += [cosine, sine]
            cosine, sine = trig(freq, offsets, side)
            extra = np.zeros((2, pad_rows if h == 0 else 0, stamp))
            if slab == 0 and h == 0:
                nyq_cos, nyq_sin = trig(np.array([side // 2]), offsets, side)
                extra[0, 0] = nyq_cos[0]
                extra[1, 0] = -nyq_sin[0]
            own += [cosine, extra[0], -sine, extra[1]]
        stamp_cols.append(np.concatenate(own))
    row_hi, row_lo = numpy_halves(np.stack([np.concatenate(part) for part in rows]))
    cosine, sine = trig(whole, whole, side)
    col_hi, col_lo = numpy_halves(np.concatenate([cosine, sine], axis=1))
    cosine, sine = trig(offsets, whole, side)
    hi, lo = numpy_halves(np.concatenate([cosine, sine], axis=1))
    stamp_rows = np.concatenate([hi, hi, lo])
    return row_hi, row_lo, col_hi, col_lo, np.stack(stamp_cols).astype(np.float32), stamp_rows


def split(value):
    high = value.astype(jnp.bfloat16)
    return high, (value - high.astype(jnp.float32)).astype(jnp.bfloat16)


def mul(left, right, contract=((1,), (0,))):
    return lax.dot_general(left, right, (contract, ((), ())), preferred_element_type=jnp.float32)


def kernel(
    slabs, subs, groups, img, bank, index, flux, noise, srow, scol,
    row_hi, row_lo, col_hi, col_lo, stamp_cols, stamp_rows,
    diff_out, flux_out,
    fwd_send, fwd_recv, bwd_send, bwd_recv, spec, filt_hi, filt_lo, psf, inv_sq, weight_own, weight_recv,
    quot, part, part_recv, block, full, pick_row, pick_tab, fl_send, fl_recv,
    s_fs, s_fr, s_bs, s_br, s_ws, s_wr, s_rs, s_rr, s_as, s_ar, s_xs, s_xr,
):
    f32 = jnp.float32
    epochs, slab_rows, side = img.shape
    stamps = bank.shape[0]
    half = side // (2 * slabs)
    strip = half // strips
    pair = 2 * strip
    exts = [strip + pad_rows] + [strip] * (strips - 1)
    width = side // groups
    per_dest = fl_send.shape[2]
    chunk = min(512, per_dest)
    chunks = per_dest // chunk
    tile = lax.axis_index("tile")
    sub = lax.axis_index("sub")
    me = tile * subs + sub
    zed = lax.axis_index("epoch")

    def slab_peer(step):
        other = lax.rem(me + step, slabs)
        return other, {"tile": other // subs, "sub": lax.rem(other, subs)}

    def zed_peer(step):
        other = lax.rem(zed + step, groups)
        return other, {"epoch": other}

    slab_order = sorted(range(1, slabs), key=lambda step: step % subs == 0, reverse=True)
    slab_order = [s for s in slab_order]

    barrier = pltpu.get_barrier_semaphore()
    for step in range(1, slabs):
        pl.semaphore_signal(barrier, inc=1, device_id=slab_peer(step)[1], device_id_type=MESH)
    for step in range(1, groups):
        pl.semaphore_signal(barrier, inc=1, device_id=zed_peer(step)[1], device_id_type=MESH)

    def slab_copy(send, recv, ssem, rsem, h, step):
        other, where = slab_peer(step)
        return pltpu.make_async_remote_copy(
            src_ref=send.at[h, other], dst_ref=recv.at[h, me],
            send_sem=ssem.at[step, h], recv_sem=rsem.at[step, h],
            device_id=where, device_id_type=MESH,
        )

    pixels = img[...].reshape(epochs * slab_rows, side)
    hi, lo = split(pixels)
    nt = ((1,), (1,))
    for h in range(strips):
        fwd = mul(row_hi[h], hi, nt) + mul(row_hi[h], lo, nt) + mul(row_lo[h], hi, nt)
        for s in range(slabs):
            for e in range(epochs):
                fwd_send[h, s, e] = fwd[s * pair : (s + 1) * pair, e * slab_rows : (e + 1) * slab_rows]
        if h == 0:
            pl.semaphore_wait(barrier, slabs - 1 + groups - 1)
        for step in slab_order:
            slab_copy(fwd_send, fwd_recv, s_fs, s_fr, h, step).start()
        fwd_recv[h, me] = fwd_send[h, me]

    lane = lax.broadcasted_iota(jnp.int32, (8, 128), 1)
    wsum = jnp.zeros((8, 128), f32)
    for e in range(epochs):
        ratio = jnp.full((8, 128), flux[e], f32) / jnp.full((8, 128), noise[e], f32)
        wsum = wsum + jnp.where(lane == index[e], ratio * ratio, 0.0)
    weight_own[...] = wsum
    for step in range(1, groups):
        _, where = zed_peer(step)
        pltpu.make_async_remote_copy(
            src_ref=weight_own, dst_ref=weight_recv.at[step],
            send_sem=s_ws.at[step], recv_sem=s_wr.at[step], device_id=where, device_id_type=MESH,
        ).start()

    cols = stamp_cols[me]
    batch = 4 if stamps % 4 == 0 else 1
    group_lane = lax.broadcasted_iota(jnp.int32, (batch * cols.shape[0], 3 * bank.shape[1]), 1)
    middle = (group_lane >= bank.shape[1]) & (group_lane < 2 * bank.shape[1])

    def stamp_body(group, carry):
        parts = []
        for i in range(batch):
            k = group * batch + i
            stamp = bank[k]
            total = jnp.sum(jnp.sum(stamp, axis=1, keepdims=True), axis=0, keepdims=True)
            stamp = stamp / total
            square = jnp.sum(jnp.sum(stamp * stamp, axis=1, keepdims=True), axis=0, keepdims=True)
            inv_sq[k] = jnp.broadcast_to(1.0 / square, (8, 128))
            wide = jnp.concatenate([stamp, stamp, stamp], axis=0)
            parts.append(
                lax.dot_general(
                    cols, wide, (((1,), (1,)), ((), ())),
                    precision=lax.Precision.HIGHEST, preferred_element_type=f32,
                )
            )
        part_spec = jnp.concatenate(parts, axis=0)
        high = part_spec.astype(jnp.bfloat16).astype(f32)
        left = jnp.where(middle, part_spec - high, high).astype(jnp.bfloat16)
        every = mul(left, stamp_rows[...])
        for i in range(batch):
            base = i * cols.shape[0]
            for h, ext in enumerate(exts):
                re, im = every[base : base + ext], every[base + ext : base + 2 * ext]
                base += 2 * ext
                psf[h, group * batch + i, 0, :ext] = re[:, :side] + im[:, side:]
                psf[h, group * batch + i, 1, :ext] = im[:, :side] - re[:, side:]
        return carry

    lax.fori_loop(0, stamps // batch, stamp_body, 0)

    for step in range(1, groups):
        _, where = zed_peer(step)
        pltpu.make_async_remote_copy(
            src_ref=weight_own, dst_ref=weight_recv.at[step],
            send_sem=s_ws.at[step], recv_sem=s_wr.at[step], device_id=where, device_id_type=MESH,
        ).wait()
        wsum = wsum + weight_recv[step]
    for h, ext in enumerate(exts):
        total_q = jnp.full((ext, side), reg_floor, f32)
        for k in range(stamps):
            re = psf[h, k, 0, :ext]
            im = psf[h, k, 1, :ext]
            total_q = total_q + wsum[0:1, k : k + 1] * (re * re + im * im)
        quot[h, 0, :ext] = total_q
        quot[h, 1, :ext] = jnp.sqrt(total_q)

    mine = pl.ds(pl.multiple_of(me * pair, pair), pair)
    pixel = lax.broadcasted_iota(jnp.int32, (side, chunk), 0)

    def pick_body(c, carry):
        at = pl.ds(pl.multiple_of(c * chunk, chunk), chunk)
        pick_row[c] = jnp.where(pixel == srow[:, at], 1.0, 0.0).astype(jnp.bfloat16)
        hot = jnp.where(pixel == scol[:, at], 1.0, 0.0).astype(jnp.bfloat16)
        for h in range(strips):
            pick_tab[c, h * pair : (h + 1) * pair] = mul(row_hi[h, mine, :], hot) + mul(row_lo[h, mine, :], hot)
        return carry

    picks = chunks * slabs

    first = (lax.broadcasted_iota(jnp.int32, (strip, side), 0) == 0) & (me == 0)
    first_ext = (lax.broadcasted_iota(jnp.int32, (pad_rows, side), 0) == 0) & (me == 0)

    def reduce_copy(h, step):
        other, where = zed_peer(step)
        rows = pl.ds(0, exts[h])
        return pltpu.make_async_remote_copy(
            src_ref=part.at[h, other, :, rows], dst_ref=part_recv.at[h, step, :, rows],
            send_sem=s_rs.at[step, h], recv_sem=s_rr.at[step, h], device_id=where, device_id_type=MESH,
        )

    def gather_copy(h, step):
        other, where = zed_peer(step)
        rows = pl.ds(0, exts[h])
        return pltpu.make_async_remote_copy(
            src_ref=block.at[h, :, rows], dst_ref=full.at[h, zed, :, rows],
            send_sem=s_as.at[step, h], recv_sem=s_ar.at[step, h], device_id=where, device_id_type=MESH,
        )

    def forward(h):
        ext = exts[h]
        for step in slab_order:
            slab_copy(fwd_send, fwd_recv, s_fs, s_fr, h, step).wait()
        lines = [fwd_recv[h, s].reshape(epochs * pair, slab_rows) for s in range(slabs)]
        if slab_rows % 128 == 0:
            pieces = [(0, side, jnp.concatenate(lines, axis=1))]
        else:
            pieces = [(s * slab_rows, slab_rows, lines[s]) for s in range(slabs)]
        every = None
        for start, size, value in pieces:
            hi, lo = split(value)
            high_tab = col_hi[start : start + size, :]
            term = mul(hi, high_tab) + mul(lo, high_tab) + mul(hi, col_lo[start : start + size, :])
            every = term if every is None else every + term
        num_re = jnp.zeros((ext, side), f32)
        num_im = jnp.zeros((ext, side), f32)
        for e in range(epochs):
            both = every[e * pair : (e + 1) * pair]
            a_re, b_re = both[:strip, :side], both[:strip, side:]
            a_im, b_im = both[strip:, :side], both[strip:, side:]
            if h == 0:
                img_re = jnp.concatenate(
                    [a_re + jnp.where(first, 0.0, b_im), jnp.where(first_ext, a_im[:pad_rows], 0.0)], axis=0
                )
                img_im = jnp.concatenate(
                    [jnp.where(first, 0.0, a_im) - b_re, jnp.where(first_ext, -b_im[:pad_rows], 0.0)], axis=0
                )
            else:
                img_re = a_re + b_im
                img_im = a_im - b_re
            spec[h, e, 0, :ext] = img_re
            spec[h, e, 1, :ext] = img_im
            psf_re = psf[h, index[e], 0, :ext]
            psf_im = psf[h, index[e], 1, :ext]
            sig = jnp.full((1, side), noise[e], f32)
            weight = jnp.full((1, side), flux[e], f32) / (sig * sig)
            num_re = num_re + weight * (psf_re * img_re + psf_im * img_im)
            num_im = num_im + weight * (psf_re * img_im - psf_im * img_re)
        for g in range(groups):
            part[h, g, 0, :ext] = num_re[:, g * width : (g + 1) * width]
            part[h, g, 1, :ext] = num_im[:, g * width : (g + 1) * width]
        for step in range(1, groups):
            reduce_copy(h, step).start()

    def reduce(h):
        ext = exts[h]
        total = part[h, zed, :, :ext]
        for step in range(1, groups):
            reduce_copy(h, step).wait()
            total = total + part_recv[h, step, :, :ext]
        block[h, :, :ext] = total
        for step in range(1, groups):
            gather_copy(h, step).start()
        full[h, zed, :, :ext] = total

    def back(h, planes_re, planes_im):
        ext = exts[h]
        hi, lo = split(jnp.concatenate([x for re_im in zip(planes_re, planes_im) for x in re_im], axis=0))
        every = mul(hi, col_hi[...]) + mul(lo, col_hi[...]) + mul(hi, col_lo[...])
        out = []
        for e in range(epochs):
            both = every[e * 2 * ext : (e + 1) * 2 * ext]
            g_re = both[:ext, :side] - both[ext:, side:]
            g_im = both[ext:, :side] + both[:ext, side:]
            if h == 0:
                head = jnp.where(first_ext, g_re[strip:], g_im[:pad_rows])
                out.append(jnp.concatenate([g_re[:strip], head, g_im[pad_rows:strip]], axis=0))
            else:
                out.append(jnp.concatenate([g_re, g_im], axis=0))
        return out

    def differences(h):
        ext = exts[h]
        for step in range(1, groups):
            gather_copy(h, step).wait()
        root_q = quot[h, 1, :ext]
        inv_root = 1.0 / root_q
        templ_re = jnp.concatenate([full[h, g, 0, :ext] for g in range(groups)], axis=1) * inv_root
        templ_im = jnp.concatenate([full[h, g, 1, :ext] for g in range(groups)], axis=1) * inv_root
        norm = jnp.full((ext, side), 2.0 / (side * side), f32)
        if h == 0:
            line = lax.broadcasted_iota(jnp.int32, (ext, side), 0)
            norm = jnp.where(((line == 0) & (me == 0)) | (line >= strip), 1.0 / (side * side), norm)
        planes_re, planes_im = [], []
        for e in range(epochs):
            psf_re = psf[h, index[e], 0, :ext]
            psf_im = psf[h, index[e], 1, :ext]
            img_re = spec[h, e, 0, :ext]
            img_im = spec[h, e, 1, :ext]
            sig = jnp.full((1, side), noise[e], f32)
            scale = jnp.full((1, side), flux[e], f32)
            power = psf_re * psf_re + psf_im * psf_im
            inv = norm / jnp.sqrt(sig * sig * quot[h, 0, :ext] + scale * scale * power + reg_floor)
            d_re = (root_q * img_re - scale * (psf_re * templ_re - psf_im * templ_im)) * inv
            d_im = (root_q * img_im - scale * (psf_re * templ_im + psf_im * templ_re)) * inv
            spec[h, e, 0, :ext] = d_re
            spec[h, e, 1, :ext] = d_im
            planes_re.append(d_re)
            planes_im.append(d_im)
        for e, plane in enumerate(back(h, planes_re, planes_im)):
            for s in range(slabs):
                bwd_send[h, s, e] = plane[:, s * slab_rows : (s + 1) * slab_rows]
        for step in slab_order:
            slab_copy(bwd_send, bwd_recv, s_bs, s_br, h, step).start()
        bwd_recv[h, me] = bwd_send[h, me]

    def filtered(h):
        ext = exts[h]
        planes_re, planes_im = [], []
        for e in range(epochs):
            psf_re = psf[h, index[e], 0, :ext]
            psf_im = psf[h, index[e], 1, :ext]
            d_re = spec[h, e, 0, :ext]
            d_im = spec[h, e, 1, :ext]
            inv = inv_sq[index[e]][0:1, 0:1]
            planes_re.append((d_re * psf_re + d_im * psf_im) * inv)
            planes_im.append((d_im * psf_re - d_re * psf_im) * inv)
        for e, plane in enumerate(back(h, planes_re, planes_im)):
            hi, lo = split(plane)
            at = (e * strips + h) * pair
            filt_hi[at : at + pair, :] = hi
            filt_lo[at : at + pair, :] = lo

    def final(h):
        for step in slab_order:
            slab_copy(bwd_send, bwd_recv, s_bs, s_br, h, step).wait()
        tn = ((0,), (0,))
        for e in range(epochs):
            hi, lo = split(bwd_recv[h, :, e].reshape(slabs * pair, slab_rows))
            out = mul(hi, row_hi[h], tn) + mul(lo, row_hi[h], tn) + mul(hi, row_lo[h], tn)
            diff_out[e] = out if h == 0 else diff_out[e] + out

    picks = chunks * slabs
    forward(0)
    lax.fori_loop(0, picks // 2, pick_body, 0)
    for h in range(1, strips):
        forward(h)
        reduce(h - 1)
    lax.fori_loop(picks // 2, picks, pick_body, 0)
    reduce(strips - 1)
    for h in range(strips):
        differences(h)
        filtered(h)

    def flux_body(c, carry):
        got = mul(filt_hi[...], pick_row[c]) + mul(filt_lo[...], pick_row[c])
        got = got.reshape(epochs, 2 * half, chunk) * pick_tab[c][None]
        fl_send[c // chunks, :, pl.ds(pl.multiple_of(lax.rem(c, chunks) * chunk, chunk), chunk)] = jnp.sum(got, axis=1)
        return carry

    lax.fori_loop(0, chunks * slabs, flux_body, 0)
    for step in slab_order:
        other, where = slab_peer(step)
        pltpu.make_async_remote_copy(
            src_ref=fl_send.at[other], dst_ref=fl_recv.at[step],
            send_sem=s_xs.at[step], recv_sem=s_xr.at[step], device_id=where, device_id_type=MESH,
        ).start()

    for h in range(strips):
        final(h)

    total = fl_send[me]
    for step in slab_order:
        other, where = slab_peer(step)
        pltpu.make_async_remote_copy(
            src_ref=fl_send.at[other], dst_ref=fl_recv.at[step],
            send_sem=s_xs.at[step], recv_sem=s_xr.at[step], device_id=where, device_id_type=MESH,
        ).wait()
        total = total + fl_recv[step]
    flux_out[...] = total


def shards(slabs, subs, groups, tables, images, bank, index, flux, noise, src_row, src_col):
    epochs, slab_rows, side = images.shape
    stamps, stamp, _ = bank.shape
    sources = src_row.shape[0]
    half = side // (2 * slabs)
    ext = half // strips + pad_rows
    width = side // groups
    per_dest = sources // slabs
    chunk = min(512, per_dest)
    f32 = jnp.float32
    vmem = pl.BlockSpec(memory_space=pltpu.VMEM)
    smem = pl.BlockSpec(memory_space=pltpu.SMEM)
    dma = pltpu.SemaphoreType.DMA
    plane = pltpu.VMEM((strips, slabs, epochs, 2 * half // strips, slab_rows), f32)
    return pl.pallas_call(
        functools.partial(kernel, slabs, subs, groups),
        out_shape=(
            jax.ShapeDtypeStruct((epochs, slab_rows, side), f32),
            jax.ShapeDtypeStruct((epochs, per_dest), f32),
        ),
        in_specs=[vmem, vmem, smem, smem, smem] + [vmem] * 8,
        out_specs=(vmem, vmem),
        scratch_shapes=[
            plane, plane, plane, plane,
            pltpu.VMEM((strips, epochs, 2, ext, side), f32),
            pltpu.VMEM((epochs * 2 * half, side), jnp.bfloat16),
            pltpu.VMEM((epochs * 2 * half, side), jnp.bfloat16),
            pltpu.VMEM((strips, stamps, 2, ext, side), f32),
            pltpu.VMEM((stamps, 8, 128), f32),
            pltpu.VMEM((8, 128), f32),
            pltpu.VMEM((groups, 8, 128), f32),
            pltpu.VMEM((strips, 2, ext, side), f32),
            pltpu.VMEM((strips, groups, 2, ext, width), f32),
            pltpu.VMEM((strips, groups, 2, ext, width), f32),
            pltpu.VMEM((strips, 2, ext, width), f32),
            pltpu.VMEM((strips, groups, 2, ext, width), f32),
            pltpu.VMEM((sources // chunk, side, chunk), jnp.bfloat16),
            pltpu.VMEM((sources // chunk, 2 * half, chunk), f32),
            pltpu.VMEM((slabs, epochs, per_dest), f32),
            pltpu.VMEM((slabs, epochs, per_dest), f32),
            dma((slabs, strips)), dma((slabs, strips)), dma((slabs, strips)), dma((slabs, strips)),
            dma((groups,)), dma((groups,)),
            dma((groups, strips)), dma((groups, strips)), dma((groups, strips)), dma((groups, strips)),
            dma((slabs,)), dma((slabs,)),
        ],
        compiler_params=pltpu.CompilerParams(
            collective_id=0, has_side_effects=True, vmem_limit_bytes=60 * 1024 * 1024
        ),
        name="zogy",
    )(images, bank, index, flux, noise, src_row.reshape(1, sources), src_col.reshape(1, sources), *tables)


def solution(mesh):
    subs = mesh.shape["sub"]
    slabs = mesh.shape["tile"] * subs
    groups = mesh.shape["epoch"]
    in_specs = (
        P(("grp", "epoch"), ("tile", "sub"), None),
        P(),
        P(("grp", "epoch")),
        P(("grp", "epoch")),
        P(("grp", "epoch")),
        P("grp"),
        P("grp"),
    )
    out_specs = (P(("grp", "epoch"), ("tile", "sub"), None), P(("grp", "epoch"), ("tile", "sub")))

    def run(images, bank, index, flux, noise, src_row, src_col):
        tables = make_tables(images.shape[2], slabs, bank.shape[1])
        body = functools.partial(shards, slabs, subs, groups, tables)
        return jax.shard_map(body, mesh=mesh, in_specs=in_specs, out_specs=out_specs, check_vma=False)(
            images, bank, index, flux, noise, src_row, src_col
        )

    return run
```

time: 54 us -> 49.4 us (0.915)
  Pallas kernels: 50.3 us -> 45.4 us
    pallas_call x1, Pallas kernels: 50.3 us -> 45.4 us  [shards(): pl.pallas_call(functools.partial(kernel, slabs, subs, groups), out_shape=...]
where the time goes in v2:
time: 49.4 us; the launch traced here: 48.9 us
  Pallas kernels  45.4 us (92%)
  local copies, waits for them, and re-layouts  2.88 us (6%)
  between operations  0.65 us (1%)
    pallas_call x1, Pallas kernels, shards(): pl.pallas_call(functools.partial(kernel, slabs, subs, groups), out_shape=...  45.4 us
    unnamed x4, local copies, waits for them, and re-layouts  2.88 us

profile of v2, /device:TPU:0, one launch (start us, length us, event | category | flops | bytes accessed | tf_op | source)
XLA Modules:
  0.0 48.9 jit_solution(5088660151157821420)
XLA Ops:
  0.6 45.4 %zogy.1 = (f32[4,128,512]{2,1,0:T(8,128)}, f32[4,1024]{1,0:T(4,128)}) custom-call(f32[4,128,512]{2,1,0:T(8,128)} %img.1, f32[16,16,16]{2,1,0:T(8,128)} %bank.1, s32[4]{0:T(128)} %index.1, f32[4]{0:T(128)} %flux.1, f32[4]{0:T(128)} %noise.1, s32[1,4096]{1,0:T(1,128)} %bitcast.2, s32[1,4096]{1,0:T(1,128)} %bitcast.3, ...), custom_call_target="tpu_custom_call" | custom-call | tf_op jit(solution)/shard_map/zogy/pallas_call | solution.py:417
  46.1 0.0 copy-start
  46.1 2.3 %copy.17 = f32[4,128,512]{2,1,0:T(8,128)} copy(f32[4,128,512]{2,1,0:T(8,128)} %get-tuple-element.4) | data formatting | bytes 2097152
  48.3 0.0 copy-done
  48.3 0.6 %copy.18 = f32[4,1024]{1,0:T(4,128)} copy(f32[4,1024]{1,0:T(4,128)S(1)} %copy-done) | data formatting | bytes 32768
Async XLA Ops:
  46.1 2.3 %copy-start = (f32[4,1024]{1,0:T(4,128)S(1)}, f32[4,1024]{1,0:T(4,128)}, u32[]{:S(2)}) copy-start(f32[4,1024]{1,0:T(4,128)} %get-tuple-element.5) | copy-start | bytes 49156

commit v3 on v2

--- a/solution.py
+++ b/solution.py
@@ -202,8 +202,9 @@
         at = pl.ds(pl.multiple_of(c * chunk, chunk), chunk)
         pick_row[c] = jnp.where(pixel == srow[:, at], 1.0, 0.0).astype(jnp.bfloat16)
         hot = jnp.where(pixel == scol[:, at], 1.0, 0.0).astype(jnp.bfloat16)
-        for h in range(strips):
-            pick_tab[c, h * pair : (h + 1) * pair] = mul(row_hi[h, mine, :], hot) + mul(row_lo[h, mine, :], hot)
+        tables = [row_hi[h, mine, :] for h in range(strips)] + [row_lo[h, mine, :] for h in range(strips)]
+        got = mul(jnp.concatenate(tables, axis=0), hot)
+        pick_tab[c] = got[: 2 * half] + got[2 * half :]
         return carry
 
     picks = chunks * slabs

time: 49.4 us -> 49.4 us (level)
  no operation moved by 1% of the time
where the time goes in v3:
time: 49.4 us; the launch traced here: 48.9 us
  Pallas kernels  45.4 us (92%)
  local copies, waits for them, and re-layouts  2.88 us (6%)
  between operations  0.65 us (1%)
    pallas_call x1, Pallas kernels, shards(): pl.pallas_call(functools.partial(kernel, slabs, subs, groups), out_shape=...  45.4 us
    unnamed x4, local copies, waits for them, and re-layouts  2.88 us

profile of v3, /device:TPU:0, one launch (start us, length us, event | category | flops | bytes accessed | tf_op | source)
XLA Modules:
  0.0 48.9 jit_solution(16001433690264343005)
XLA Ops:
  0.6 45.4 %zogy.1 = (f32[4,128,512]{2,1,0:T(8,128)}, f32[4,1024]{1,0:T(4,128)}) custom-call(f32[4,128,512]{2,1,0:T(8,128)} %img.1, f32[16,16,16]{2,1,0:T(8,128)} %bank.1, s32[4]{0:T(128)} %index.1, f32[4]{0:T(128)} %flux.1, f32[4]{0:T(128)} %noise.1, s32[1,4096]{1,0:T(1,128)} %bitcast.2, s32[1,4096]{1,0:T(1,128)} %bitcast.3, ...), custom_call_target="tpu_custom_call" | custom-call | tf_op jit(solution)/shard_map/zogy/pallas_call | solution.py:418
  46.1 0.0 copy-start
  46.1 2.3 %copy.17 = f32[4,128,512]{2,1,0:T(8,128)} copy(f32[4,128,512]{2,1,0:T(8,128)} %get-tuple-element.4) | data formatting | bytes 2097152
  48.3 0.0 copy-done
  48.3 0.6 %copy.18 = f32[4,1024]{1,0:T(4,128)} copy(f32[4,1024]{1,0:T(4,128)S(1)} %copy-done) | data formatting | bytes 32768
Async XLA Ops:
  46.1 2.3 %copy-start = (f32[4,1024]{1,0:T(4,128)S(1)}, f32[4,1024]{1,0:T(4,128)}, u32[]{:S(2)}) copy-start(f32[4,1024]{1,0:T(4,128)} %get-tuple-element.5) | copy-start | bytes 49156
